TPU v7x, 32 devices: a whole 2x2x4 slice. The times are simulated.
32 devices in a mesh: pair: 2 (over x), blk: 8 (over z, y), group: 2 (over core).
Axes of the slice: x: 2, y: 2, z: 4, core: 2. Of those that a mesh axis runs over, the one named last changes fastest.
Arguments:
- codes: int32 [32, 1536, 256], P(('pair', 'blk', 'group')), may hold values from 0 to 255
- scales: int32 [32, 1536, 8], P(('pair', 'blk', 'group')), may hold values from -7 to 0
- inputs: bfloat16 [4096, 1536], P(('pair', 'blk', 'group')), may hold values from -6 to 6
- cotangent: bfloat16 [4096, 256], P(('pair', 'blk', 'group')), may hold values from -6 to 6
Outputs:
- earlier_grad: float32 [1536, 256], replicated
- current_grad: float32 [1536, 256], replicated
All inputs are finite; a program needn't handle non-finite values.
Results may differ from a plain program's by a relative error of at most 0.0003.
Values sent between devices are 32-bit elements; how exact they have to be, the bound alone decides.
No kernel may reach another device: no remote copies, remote signals or barrier semaphores. Data moves between devices by JAX's collectives and lax.ppermute only.
A program may use at most 64 MiB of HBM per device.

v0:
```python
import jax
import jax.numpy as jnp
from jax import lax
from jax.sharding import PartitionSpec as P


def decode(codes, scales):
    codes = codes[0]
    scales = scales[0]
    rows, width = codes.shape
    sign = 1.0 - 2.0 * (codes // 128).astype(jnp.float32)
    field = codes // 8 % 16
    mant = (codes % 8).astype(jnp.float32)
    frac = jnp.where(field > 0, 8.0 + mant, mant)
    power = jnp.where(field > 0, field, 1) - 10
    expo = power.reshape(rows, scales.shape[1], width // scales.shape[1]) + scales[:, :, None]
    return sign * frac * jnp.exp2(expo.reshape(rows, width).astype(jnp.float32))


def combine(stack, count):
    pooled = lax.psum(stack, "pair")
    share = lax.psum_scatter(pooled, "blk", scatter_dimension=1, tiled=True)
    total = lax.psum_scatter(share, "group", scatter_dimension=1, tiled=True) / count
    return lax.all_gather(total, ("blk", "group"), axis=1, tiled=True)


def key_product(inputs, cotangent):
    return lax.dot_general(
        inputs, cotangent, (((0,), (0,)), ((), ())), preferred_element_type=jnp.float32
    )


def local(codes, scales, inputs, cotangent):
    count = lax.axis_size("pair") * lax.axis_size("blk") * lax.axis_size("group")
    decoded = decode(codes, scales)
    product = key_product(inputs, cotangent)
    summed = combine(jnp.stack([decoded, product]), count)
    earlier_grad = summed[0]
    current_grad = summed[1]
    return (earlier_grad, current_grad)


def solution(mesh):
    in_specs = (
        P(("pair", "blk", "group"), None, None),
        P(("pair", "blk", "group"), None, None),
        P(("pair", "blk", "group"), None),
        P(("pair", "blk", "group"), None),
    )
    out_specs = (P(), P())
    return jax.shard_map(local, mesh=mesh, in_specs=in_specs, out_specs=out_specs, check_vma=False)
```

profile of v0, /device:TPU:0, one launch (start us, length us, event | category | flops | bytes accessed | tf_op | source)
XLA Modules:
  0.0 186.2 jit_solution(1373778970033017761)
XLA Ops:
  7.2 0.0 copy-start
  7.2 0.0 reduce-scatter.3.cloned.1.call-start
  7.2 1.0 add.58
  8.2 0.5 copy.7
  8.7 0.0 copy-start.1
  8.7 4.5 %fusion.5 = f32[1,1536,256]{2,1,0:T(8,128)S(1)} fusion(s32[1,1536,256]{2,1,0:T(8,128)S(1)} %copy.7, s32[1,1536,256]{2,1,0:T(8,128)} %param.4), kind=kLoop, calls=%fused_computation.20 | loop fusion | flops 21233664 | bytes 4718592 | tf_op jit(solution)/shard_map/mul | solution.py:17
  13.2 0.0 copy-done
  13.2 0.0 copy-done.1
  13.3 0.4 convolution_bitcast_fusion
  13.6 1.9 pad_maximum_fusion
  15.5 0.0 reduce-scatter.3.cloned.1.call-update
  15.5 0.0 reduce-scatter.5.cloned.1.call-start
  15.6 77.1 %reduce-scatter.3.cloned.1.call-done = f32[2,192,256]{2,1,0:T(8,128)} async-done(((f32[2,1536,256]{2,1,0:T(8,128)}), f32[2,192,256]{2,1,0:T(8,128)}) %reduce-scatter.3.cloned.1.call-update) | async-done | bytes 393232 | tf_op jit(solution)/shard_map/reduce_scatter | solution.py:22
  92.7 0.0 reduce-scatter.5.cloned.1.call-update
  92.7 0.0 all-reduce.2.cloned.1.call-start
  92.8 9.1 %reduce-scatter.5.cloned.1.call-done = f32[2,96,256]{2,1,0:T(8,128)} async-done(((f32[2,192,256]{2,1,0:T(8,128)}), f32[2,96,256]{2,1,0:T(8,128)}) %reduce-scatter.5.cloned.1.call-update) | async-done | bytes 196624 | tf_op jit(solution)/shard_map/reduce_scatter | solution.py:23
  101.9 0.0 all-reduce.2.cloned.1.call-update
  101.9 0.0 all-gather.2.cloned.1.call-start
  102.0 25.8 %all-reduce.2.cloned.1.call-done = f32[2,96,256]{2,1,0:T(8,128)} async-done(((f32[2,96,256]{2,1,0:T(8,128)}), f32[2,96,256]{2,1,0:T(8,128)}) %all-reduce.2.cloned.1.call-update) | async-done | bytes 196624 | tf_op jit(solution)/shard_map/psum | solution.py:21
  127.7 1.6 broadcast_multiply_fusion
  129.3 0.0 all-gather.2.cloned.1.call-update
  129.4 46.6 %all-gather.2.cloned.1.call-done = f32[2,1536,256]{2,1,0:T(8,128)} async-done(((f32[2,96,256]{2,1,0:T(8,128)}), f32[2,1536,256]{2,1,0:T(8,128)}) %all-gather.2.cloned.1.call-update) | async-done | bytes 3145744 | tf_op jit(solution)/shard_map/all_gather | solution.py:24
  176.0 3.7 %slice_bitcast_fusion = (f32[1536,256]{1,0:T(8,128)}, f32[1536,256]{1,0:T(8,128)}) fusion(f32[2,1536,256]{2,1,0:T(8,128)} %all-gather.2.cloned.1.call-done), kind=kLoop, calls=%fused_computation.28 | loop fusion | bytes 6291456 | tf_op jit(solution)/shard_map/squeeze | solution.py:39
Async XLA Ops:
  7.2 6.1 %copy-start = (bf16[128,1536]{1,0:T(8,128)(2,1)S(1)}, bf16[128,1536]{1,0:T(8,128)(2,1)}, u32[]{:S(2)}) copy-start(bf16[128,1536]{1,0:T(8,128)(2,1)} %param.6) | copy-start | bytes 1179652
  7.2 85.5 %reduce-scatter.3.cloned.1.call-start = ((), (), s32[]{:S(2)}) async-start(), calls=%async_computation.3 | async-start | bytes 3538944 | tf_op jit(solution)/shard_map/reduce_scatter | solution.py:22
  8.7 4.5 %copy-start.1 = (bf16[128,256]{1,0:T(8,128)(2,1)S(1)}, bf16[128,256]{1,0:T(8,128)(2,1)}, u32[]{:S(2)}) copy-start(bf16[128,256]{1,0:T(8,128)(2,1)} %param.7) | copy-start | bytes 196612
  15.5 86.4 %reduce-scatter.5.cloned.1.call-start = ((), (), s32[]{:S(2)}) async-start(), calls=%async_computation.4 | async-start | bytes 589824 | tf_op jit(solution)/shard_map/reduce_scatter | solution.py:23
  92.7 35.0 %all-reduce.2.cloned.1.call-start = ((), (), s32[]{:S(2)}) async-start(), calls=%async_computation.5 | async-start | bytes 393216 | tf_op jit(solution)/shard_map/psum | solution.py:21
  101.9 74.0 %all-gather.2.cloned.1.call-start = ((), (), s32[]{:S(2)}) async-start(), calls=%async_computation.2 | async-start | bytes 3342336 | tf_op jit(solution)/shard_map/all_gather | solution.py:24
Sparse Core Ops, SparseCore 0:
  15.7 77.0 reduce-scatter.2
  94.9 6.8 reduce-scatter.4
  104.2 23.5 all-reduce.1
  130.4 45.4 all-gather.1
where the time goes:
time: 186 us
  waiting for transfers between devices  159 us (85%)
  between operations  13.8 us (7%)
  other arithmetic  7.97 us (4%)
  local copies, waits for them, and re-layouts  5.23 us (3%)
    reduce_scatter x1, waiting for transfers between devices, combine(): share = lax.psum_scatter(pooled, 'blk', scatter_dimension=1, tiled=True)  77.1 us
    all_gather x1, waiting for transfers between devices, combine(): return lax.all_gather(total, ('blk', 'group'), axis=1, tiled=True)  46.6 us
    psum x1, waiting for transfers between devices, combine(): pooled = lax.psum(stack, 'pair')  25.8 us
    reduce_scatter x1, waiting for transfers between devices, combine(): lax.psum_scatter(share, 'group', scatter_dimension=1, tiled=True) / count  9.11 us
    mul x1, other arithmetic, decode(): return sign * frac * jnp.exp2(expo.reshape(rows, width).astype(jnp.float32))  4.5 us
    squeeze x1, local copies, waits for them, and re-layouts, local(): current_grad = summed[1]  3.74 us
  transfers between devices with their start and end apart: 4, of which 4 were waited for; matrix products, arithmetic and copies ran while one was open for 0% of the time, Pallas kernels for 0%

commit v1 on v0

v1 whole, which is shorter than its diff:
```python
import functools

import jax
import jax.numpy as jnp
from jax import lax
from jax.experimental import pallas as pl
from jax.experimental.pallas import tpu as pltpu
from jax.sharding import PartitionSpec as P


AXES = ("pair", "blk", "group")
CHUNKS = (((0, 0, 8),), ((0, 8, 12), (1, 0, 4)), ((1, 4, 12),))
PARTS = 12
ROUTES = (
    ((0, 2, 1, 3), (1, 0, 2, 3)),
    ((1, 2, 0, 3), (2, 0, 3, 1)),
    ((2, 1, 0, 3), (0, 2, 1, 3)),
)
SUBLANES = 8
VMEM = pl.BlockSpec(memory_space=pltpu.VMEM)
HBM = pl.BlockSpec(memory_space=pltpu.HBM)
GRANT = 8 * 1024 * 1024


def bits_of(size):
    return size.bit_length() - 1


def routes(shape, order):
    group = [("group", b) for b in range(bits_of(shape["group"]))]
    bits = [(axis, b) for axis in ("pair", "blk") for b in range(bits_of(shape[axis]))] + group[1:]
    both = [[bits[k] for k in one if k < len(bits)] + bits[len(one):] for one in order]
    return [(group[0], group[0])] + list(zip(*both))


def side_of(shape, index):
    total = 0
    for axis in AXES:
        for b in range(bits_of(shape[axis])):
            total = total + ((index[axis] >> b) & 1)
    return total % 2


def pairs_of(shape, route, first):
    sizes = [shape[a] for a in AXES]
    out = []
    for i in range(sizes[0] * sizes[1] * sizes[2]):
        index = {"group": i % sizes[2], "blk": i // sizes[2] % sizes[1], "pair": i // sizes[2] // sizes[1]}
        axis, bit = route[side_of(shape, index)]
        index[axis] ^= 1 << bit
        if not first:
            index["group"] ^= 1
        out.append((i, (index["pair"] * sizes[1] + index["blk"]) * sizes[2] + index["group"]))
    return out


def side_now(shape):
    return side_of(shape, {axis: lax.axis_index(axis) for axis in AXES})


def bit_now(shape, route):
    values = [(lax.axis_index(axis) >> bit) & 1 for axis, bit in route]
    if route[0] == route[1]:
        return values[0]
    return jnp.where(side_now(shape) == 0, values[0], values[1])


def call(body, outs, *args, hbm_in=(), hbm_out=False, alias=None, scratch=()):
    ins = [HBM if i in hbm_in else VMEM for i in range(len(args))]
    args = [pltpu.with_memory_space_constraint(a, pltpu.HBM if i in hbm_in else pltpu.VMEM) for i, a in enumerate(args)]
    make_out, spec = (pltpu.HBM, HBM) if hbm_out else (pltpu.VMEM, VMEM)
    return list(pl.pallas_call(
        body, out_shape=[make_out(s, d) for s, d in outs], in_specs=ins, out_specs=[spec] * len(outs),
        scratch_shapes=list(scratch), input_output_aliases=alias or {},
        compiler_params=pltpu.CompilerParams(vmem_limit_bytes=GRANT),
    )(*args))


def aligned(start, size, to=SUBLANES):
    return pl.ds(pl.multiple_of(start, to), size)


def product_body(shape, plan, x_hbm, c_hbm, codes_hbm, scales_hbm, *refs):
    n = len(refs) - 5
    results, codes_ref, scales_ref = refs[:n], refs[n], refs[n + 1]
    x_ref, c_ref, sem = refs[n + 2:]
    copies = [pltpu.make_async_copy(a, b, sem.at[k]) for k, (a, b) in enumerate(
        ((x_hbm, x_ref), (c_hbm, c_ref), (scales_hbm, scales_ref), (codes_hbm, codes_ref)))]
    for copy in copies:
        copy.start()
    copies[0].wait()
    copies[1].wait()
    side = side_now(shape)
    half = x_ref.shape[1] // 2
    for k, to, start, rows in plan:
        for ref, of in ((results[2 * k], 1 - side), (results[2 * k + 1], side)):
            ref[pl.ds(to, rows), :] = lax.dot_general(
                x_ref[:, aligned(of * half + start, rows, 128)], c_ref[...], (((0,), (0,)), ((), ())),
                preferred_element_type=jnp.float32)
    copies[2].wait()
    copies[3].wait()


def decode_body(shape, plan, codes_ref, scales_ref, *refs):
    away_ref, keep_ref = refs[-2:]
    side = side_now(shape)
    height, width = codes_ref.shape
    blocks = scales_ref.shape[0]
    owner = lax.broadcasted_iota(jnp.int32, (blocks, width), 1) // (width // blocks)
    spread = (owner == lax.broadcasted_iota(jnp.int32, (blocks, width), 0)).astype(jnp.float32).astype(jnp.bfloat16)
    for to, start, rows in plan:
        for ref, of in ((away_ref, 1 - side), (keep_ref, side)):
            first = of * (height // 2) + start
            unit = jnp.left_shift(1, scales_ref[:, aligned(first, rows, 128)] + 7).astype(jnp.float32) * 2.0**-17
            unit = lax.dot_general(
                unit.astype(jnp.bfloat16), spread, (((0,), (0,)), ((), ())), preferred_element_type=jnp.float32)
            codes = codes_ref[aligned(first, rows), :]
            field = (codes >> 3) & 15
            mant = codes & 7
            frac = jnp.where(field > 0, mant + 8, mant)
            whole = jnp.left_shift(frac, jnp.maximum(field, 1)).astype(jnp.float32)
            ref[pl.ds(to, rows), :] = jnp.where(codes > 127, -whole, whole) * unit


def split_body(shape, route, keep_ref, got_ref, away_ref, held_ref):
    half = away_ref.shape[0]
    bit = bit_now(shape, route)
    for ref, of in ((away_ref, 1 - bit), (held_ref, bit)):
        rows = aligned(of * half, half)
        ref[...] = keep_ref[rows, :] + got_ref[rows, :]


def add_body(scale, keep_ref, got_ref, out_ref):
    out_ref[...] = (keep_ref[...] + got_ref[...]) * scale


def join_body(shape, route, held_ref, got_ref, out_ref):
    half = held_ref.shape[0]
    bit = bit_now(shape, route)
    for ref, of in ((held_ref, bit), (got_ref, 1 - bit)):
        out_ref[aligned(of * half, half), :] = ref[...]


def write_body(shape, plan, n_out, *refs):
    outs, sem = refs[-n_out - 1:-1], refs[-1]
    side = side_now(shape)
    copies = []
    for k, (i, at, o, start, rows, other) in enumerate(plan):
        of = 1 - side if other else side
        to = outs[o].at[aligned(of * (outs[o].shape[0] // 2) + start, rows), :]
        copies.append(pltpu.make_async_copy(refs[i].at[pl.ds(at, rows), :], to, sem.at[k]))
        copies[-1].start()
    for copy in copies:
        copy.wait()


class Chunk:
    def __init__(self, shape, order):
        self.shape = shape
        self.steps = routes(shape, order)
        self.pairs = [pairs_of(shape, s, i == 0) for i, s in enumerate(self.steps)]
        self.scale = 1.0 / (shape["pair"] * shape["blk"] * shape["group"])
        self.undo = []
        self.turned = False

    def begin(self, away, keep):
        self.keep = keep
        self.send(away, 0)

    def send(self, x, step):
        self.got = lax.ppermute(x, AXES, self.pairs[step])
        self.step = step

    def one(self, body, keep):
        (out,) = call(body, [(keep, jnp.float32)], self.keep, self.got)
        return out

    def go(self):
        last = len(self.steps) - 1
        rows, width = self.keep.shape
        shape = self.shape
        if self.step < last and not self.turned:
            i = self.step + 1
            half = rows // 2
            if i < last and half % SUBLANES == 0:
                away, self.keep = call(functools.partial(split_body, shape, self.steps[i]),
                                       [((half, width), jnp.float32)] * 2, self.keep, self.got)
                self.undo.append(i)
                self.send(away, i)
            else:
                self.keep = self.one(functools.partial(add_body, 1.0), (rows, width))
                self.send(self.keep, i)
        elif not self.turned:
            self.keep = self.one(functools.partial(add_body, self.scale), (rows, width))
            self.turned = True
            self.send(self.keep, self.undo[-1] if self.undo else 0)
        else:
            i = self.undo.pop()
            self.keep = self.one(functools.partial(join_body, shape, self.steps[i]), (2 * rows, width))
            self.send(self.keep, self.undo[-1] if self.undo else 0)

    def ended(self):
        return self.turned and not self.undo


def make(shape):
    def local(codes, scales, inputs, cotangent):
        height, width = codes.shape[1:]
        half = height // 2
        f32 = jnp.float32
        jobs = []
        for pieces in CHUNKS:
            at = 0
            job = []
            for o, start, end in pieces:
                start, end = half * start // PARTS, half * end // PARTS
                job.append((o, at, start, end - start))
                at += end - start
            jobs.append((job, at))
        plan, outs, first = [], [], {}
        for c, (job, rows) in enumerate(jobs):
            for o, at, start, size in job:
                if o == 0:
                    if c not in first:
                        first[c] = len(outs) // 2
                        outs += [((rows, width), f32)] * 2
                    plan.append((first[c], at, start, size))
        flat, scale_rows = codes[0], scales[0].T
        vm = [((height, width), jnp.int32), (scale_rows.shape, jnp.int32)]
        got = call(functools.partial(product_body, shape, plan), outs + vm, inputs, cotangent, flat, scale_rows,
                   hbm_in=(0, 1, 2, 3),
                   scratch=[pltpu.VMEM(inputs.shape, inputs.dtype), pltpu.VMEM(cotangent.shape, cotangent.dtype),
                            pltpu.SemaphoreType.DMA((4,))])
        flat, scale_rows = got[-2:]
        chains = []
        for c, (job, rows) in enumerate(jobs):
            pair = got[2 * first[c]:2 * first[c] + 2] if c in first else []
            plan = [(at, start, size) for o, at, start, size in job if o == 1]
            if plan:
                pair = call(functools.partial(decode_body, shape, plan), [((rows, width), f32)] * 2,
                            flat, scale_rows, *pair, alias={2: 0, 3: 1} if pair else None)
            chain = Chunk(shape, ROUTES[c])
            chain.begin(*pair)
            chains.append(chain)
        while not all(chain.ended() for chain in chains):
            for chain in chains:
                if not chain.ended():
                    chain.go()
        ins = [chain.keep for chain in chains] + [chain.got for chain in chains]
        n = len(chains)
        plan = [(c + n * other, at, o, start, size, other)
                for other in (0, 1) for c, (job, _) in enumerate(jobs) for o, at, start, size in job]
        full = ((height, width), f32)
        outs = []
        for other in (0, 1):
            part = [(i - n * other, *rest) for i, *rest in plan if rest[-1] == other]
            outs = call(functools.partial(write_body, shape, part, 2), [full] * 2, *ins[n * other:n * other + n],
                        *outs, hbm_in=(n, n + 1), hbm_out=True, alias={n: 0, n + 1: 1} if outs else None,
                        scratch=[pltpu.SemaphoreType.DMA((len(part),))])
        return (outs[1], outs[0])

    return local


def solution(mesh):
    in_specs = (
        P(("pair", "blk", "group"), None, None),
        P(("pair", "blk", "group"), None, None),
        P(("pair", "blk", "group"), None),
        P(("pair", "blk", "group"), None),
    )
    out_specs = (P(), P())
    return jax.shard_map(make(dict(mesh.shape)), mesh=mesh, in_specs=in_specs, out_specs=out_specs, check_vma=False)
```

time: 186 us -> 55.8 us (0.30)
  waiting for transfers between devices: 159 us -> 9.63 us
  starting transfers between devices: 0.16 us -> 39.6 us
  between operations: 13.8 us -> 0.81 us
  other arithmetic: 7.97 us -> 0 us
  Pallas kernels: 0 us -> 5.64 us
  local copies, waits for them, and re-layouts: 5.23 us -> 0 us
    reduce_scatter x2 -> x0, waiting for transfers between devices: 86.2 us -> none  [the longest x1 77.1 us: combine(): share = lax.psum_scatter(pooled, 'blk', scatter_dimension=1, tiled=True)]
    all_gather x1 -> x0, waiting for transfers between devices: 46.6 us -> none  [combine(): return lax.all_gather(total, ('blk', 'group'), axis=1, tiled=True)]
    ppermute x0 -> x27, starting transfers between devices: none -> 39.6 us  [send(): self.got = lax.ppermute(x, AXES, self.pairs[step])]
    psum x1 -> x0, waiting for transfers between devices: 25.8 us -> none  [combine(): pooled = lax.psum(stack, 'pair')]
    ppermute x0 -> x27, waiting for transfers between devices: none -> 9.63 us  [send(): self.got = lax.ppermute(x, AXES, self.pairs[step])]
    pallas_call x0 -> x29, Pallas kernels: none -> 5.64 us  [call(): pl.pallas_call(body, out_shape=[make_out(s, d) for s, d in outs], in_spec...]
    mul x1 -> x0, other arithmetic: 4.5 us -> none  [decode(): return sign * frac * jnp.exp2(expo.reshape(rows, width).astype(jnp.float32))]
    squeeze x1 -> x0, local copies, waits for them, and re-layouts: 3.74 us -> none  [local(): current_grad = summed[1]]
  transfers between devices with their start and end apart: 4 -> 27, of which waited for: 4 -> 9; matrix products, arithmetic and copies ran while one was open for 0% -> 0% of each run, Pallas kernels for 0% -> 5%
where the time goes in v1:
time: 55.8 us; the launch traced here: 55.7 us
  starting transfers between devices  39.6 us (71%)
  waiting for transfers between devices  9.63 us (17%)
  Pallas kernels  5.64 us (10%)
  between operations  0.81 us (1%)
    ppermute x27, starting transfers between devices, send(): self.got = lax.ppermute(x, AXES, self.pairs[step])  39.6 us
    ppermute x27, waiting for transfers between devices, send(): self.got = lax.ppermute(x, AXES, self.pairs[step])  9.63 us
    pallas_call x29, Pallas kernels, call(): pl.pallas_call(body, out_shape=[make_out(s, d) for s, d in outs], in_spec...  5.64 us
  transfers between devices with their start and end apart: 27, of which 9 were waited for; matrix products, arithmetic and copies ran while one was open for 0% of the time, Pallas kernels for 5%

profile of v1, /device:TPU:0, one launch (start us, length us, event | category | flops | bytes accessed | tf_op | source)
XLA Modules:
  0.0 55.7 jit_solution(3662493783995986340)
XLA Ops:
  0.6 1.6 %shard_map.59 = (f32[512,256]{1,0:T(8,128)S(1)}, f32[512,256]{1,0:T(8,128)S(1)}, f32[512,256]{1,0:T(8,128)S(1)}, f32[512,256]{1,0:T(8,128)S(1)}, s32[1536,256]{1,0:T(8,128)S(1)}, /*index=5*/s32[8,1536]{1,0:T(8,128)S(1)}) custom-call(bf16[128,1536]{1,0:T(8,128)(2,1)} %x_hbm.1, bf16[128,256]{1,0:T(8,128)(2,1)} %c_hbm.1, s32[1536,256]{1,0:T(8,128)} %bitcast.4, ...), custom_call_target="tpu_custom_call" | custom-call | tf_op jit(solution)/shard_map/pallas_call | solution.py:72
  2.3 0.6 %collective-permute-start = (f32[512,256]{1,0:T(8,128)S(1)}, f32[512,256]{1,0:T(8,128)S(1)}, u32[]{:S(2)}, u32[]{:S(2)}) collective-permute-start(f32[512,256]{1,0:T(8,128)S(1)} %get-tuple-element.35), channel_id=1, source_target_pairs={{0,1},{1,0},{2,3},{3,2},{4,5},{5,4},{6,7},{7,6},{8,9},{9,8},{10,11... | collective-permute-start | bytes 1572872 | tf_op jit(solution)/shard_map/ppermute | solution.py:171
  2.8 0.4 shard_map.68
  3.2 0.1 collective-permute-start.9
  3.3 0.6 %shard_map.77 = (f32[512,256]{1,0:T(8,128)S(1)}, f32[512,256]{1,0:T(8,128)S(1)}) custom-call(s32[1536,256]{1,0:T(8,128)S(1)} %get-tuple-element.42.codes_ref, s32[8,1536]{1,0:T(8,128)S(1)} %get-tuple-element.43.scales_ref), custom_call_target="tpu_custom_call" | custom-call | tf_op jit(solution)/shard_map/pallas_call | solution.py:72
  3.9 0.6 collective-permute-start.18
  4.5 0.0 collective-permute-done.got_ref
  4.5 0.1 shard_map.60
  4.5 2.6 %collective-permute-start.1 = (f32[256,256]{1,0:T(8,128)S(1)}, f32[256,256]{1,0:T(8,128)S(1)}, u32[]{:S(2)}, u32[]{:S(2)}) collective-permute-start(f32[256,256]{1,0:T(8,128)S(1)} %get-tuple-element.37), channel_id=1, source_target_pairs={{0,17},{1,2},{2,1},{3,18},{4,7},{5,20},{6,23},{7,4},{8,11},{9,24},... | collective-permute-start | bytes 786440 | tf_op jit(solution)/shard_map/ppermute | solution.py:171
  7.2 0.1 shard_map.69
  7.2 1.5 %collective-permute-start.10 = (f32[256,256]{1,0:T(8,128)S(1)}, f32[256,256]{1,0:T(8,128)S(1)}, u32[]{:S(2)}, u32[]{:S(2)}) collective-permute-start(f32[256,256]{1,0:T(8,128)S(1)} %get-tuple-element.49), channel_id=1, source_target_pairs={{0,3},{1,4},{2,7},{3,0},{4,1},{5,6},{6,5},{7,2},{8,13},{9,10},{10,... | collective-permute-start | bytes 786440 | tf_op jit(solution)/shard_map/ppermute | solution.py:171
  8.7 0.1 shard_map.78
  8.8 1.5 %collective-permute-start.19 = (f32[256,256]{1,0:T(8,128)S(1)}, f32[256,256]{1,0:T(8,128)S(1)}, u32[]{:S(2)}, u32[]{:S(2)}) collective-permute-start(f32[256,256]{1,0:T(8,128)S(1)} %get-tuple-element.57), channel_id=1, source_target_pairs={{0,5},{1,16},{2,19},{3,6},{4,21},{5,0},{6,3},{7,22},{8,25},{9,12},... | collective-permute-start | bytes 786440 | tf_op jit(solution)/shard_map/ppermute | solution.py:171
  10.2 1.0 %collective-permute-done.1.got_ref = f32[256,256]{1,0:T(8,128)S(1)} collective-permute-done((f32[256,256]{1,0:T(8,128)S(1)}, f32[256,256]{1,0:T(8,128)S(1)}, u32[]{:S(2)}, u32[]{:S(2)}) %collective-permute-start.1) | collective-permute-done | bytes 262176 | tf_op jit(solution)/shard_map/ppermute | solution.py:171
  11.3 3.5 %collective-permute-start.2 = (f32[128,256]{1,0:T(8,128)S(1)}, f32[128,256]{1,0:T(8,128)S(1)}, u32[]{:S(2)}, u32[]{:S(2)}) collective-permute-start(f32[128,256]{1,0:T(8,128)S(1)} %get-tuple-element.39), channel_id=1, source_target_pairs={{0,5},{1,16},{2,19},{3,6},{4,21},{5,0},{6,3},{7,22},{8,25},{9,12},... | collective-permute-start | bytes 393224 | tf_op jit(solution)/shard_map/ppermute | solution.py:171
  14.7 1.1 %collective-permute-start.11 = (f32[128,256]{1,0:T(8,128)S(1)}, f32[128,256]{1,0:T(8,128)S(1)}, u32[]{:S(2)}, u32[]{:S(2)}) collective-permute-start(f32[128,256]{1,0:T(8,128)S(1)} %get-tuple-element.51), channel_id=1, source_target_pairs={{0,5},{1,16},{2,19},{3,6},{4,21},{5,0},{6,3},{7,22},{8,25},{9,12},... | collective-permute-start | bytes 393224 | tf_op jit(solution)/shard_map/ppermute | solution.py:171
  15.8 0.5 collective-permute-done.19.got_ref
  16.4 1.4 %collective-permute-start.20 = (f32[128,256]{1,0:T(8,128)S(1)}, f32[128,256]{1,0:T(8,128)S(1)}, u32[]{:S(2)}, u32[]{:S(2)}) collective-permute-start(f32[128,256]{1,0:T(8,128)S(1)} %get-tuple-element.59), channel_id=1, source_target_pairs={{0,3},{1,4},{2,7},{3,0},{4,1},{5,6},{6,5},{7,2},{8,13},{9,10},{10,... | collective-permute-start | bytes 393224 | tf_op jit(solution)/shard_map/ppermute | solution.py:171
  17.9 1.2 %collective-permute-start.3 = (f32[64,256]{1,0:T(8,128)S(1)}, f32[64,256]{1,0:T(8,128)S(1)}, u32[]{:S(2)}, u32[]{:S(2)}) collective-permute-start(f32[64,256]{1,0:T(8,128)S(1)} %get-tuple-element.41), channel_id=1, source_target_pairs={{0,3},{1,4},{2,7},{3,0},{4,1},{5,6},{6,5},{7,2},{8,13},{9,10},{10,... | collective-permute-start | bytes 196616 | tf_op jit(solution)/shard_map/ppermute | solution.py:171
  19.1 0.1 collective-permute-done.11.got_ref
  19.2 1.9 %collective-permute-start.12 = (f32[64,256]{1,0:T(8,128)S(1)}, f32[64,256]{1,0:T(8,128)S(1)}, u32[]{:S(2)}, u32[]{:S(2)}) collective-permute-start(f32[64,256]{1,0:T(8,128)S(1)} %get-tuple-element.53), channel_id=1, source_target_pairs={{0,17},{1,8},{2,11},{3,18},{4,13},{5,20},{6,23},{7,14},{8,1},{9,24... | collective-permute-start | bytes 196616 | tf_op jit(solution)/shard_map/ppermute | solution.py:171
  21.2 1.1 %collective-permute-start.21 = (f32[64,256]{1,0:T(8,128)S(1)}, f32[64,256]{1,0:T(8,128)S(1)}, u32[]{:S(2)}, u32[]{:S(2)}) collective-permute-start(f32[64,256]{1,0:T(8,128)S(1)} %get-tuple-element.61), channel_id=1, source_target_pairs={{0,17},{1,2},{2,1},{3,18},{4,7},{5,20},{6,23},{7,4},{8,11},{9,24},... | collective-permute-start | bytes 196616 | tf_op jit(solution)/shard_map/ppermute | solution.py:171
  22.3 2.5 %collective-permute-start.4 = (f32[64,256]{1,0:T(8,128)S(1)}, f32[64,256]{1,0:T(8,128)S(1)}, u32[]{:S(2)}, u32[]{:S(2)}) collective-permute-start(f32[64,256]{1,0:T(8,128)S(1)} %shard_map.63.keep_ref), channel_id=1, source_target_pairs={{0,9},{1,8},{2,11},{3,10},{4,13},{5,12},{6,15},{7,14},{8,1},{9,0},... | collective-permute-start | bytes 196616 | tf_op jit(solution)/shard_map/ppermute | solution.py:171
  24.9 0.8 %collective-permute-start.13 = (f32[64,256]{1,0:T(8,128)S(1)}, f32[64,256]{1,0:T(8,128)S(1)}, u32[]{:S(2)}, u32[]{:S(2)}) collective-permute-start(f32[64,256]{1,0:T(8,128)S(1)} %shard_map.72.keep_ref), channel_id=1, source_target_pairs={{0,9},{1,2},{2,1},{3,10},{4,7},{5,12},{6,15},{7,4},{8,11},{9,0},{1... | collective-permute-start | bytes 196616 | tf_op jit(solution)/shard_map/ppermute | solution.py:171
  25.7 2.1 %collective-permute-start.22 = (f32[64,256]{1,0:T(8,128)S(1)}, f32[64,256]{1,0:T(8,128)S(1)}, u32[]{:S(2)}, u32[]{:S(2)}) collective-permute-start(f32[64,256]{1,0:T(8,128)S(1)} %shard_map.81.keep_ref), channel_id=1, source_target_pairs={{0,9},{1,8},{2,11},{3,10},{4,13},{5,12},{6,15},{7,14},{8,1},{9,0},... | collective-permute-start | bytes 196616 | tf_op jit(solution)/shard_map/ppermute | solution.py:171
  27.8 1.3 %collective-permute-start.5 = (f32[64,256]{1,0:T(8,128)S(1)}, f32[64,256]{1,0:T(8,128)S(1)}, u32[]{:S(2)}, u32[]{:S(2)}) collective-permute-start(f32[64,256]{1,0:T(8,128)S(1)} %shard_map.64.held_ref), channel_id=1, source_target_pairs={{0,3},{1,4},{2,7},{3,0},{4,1},{5,6},{6,5},{7,2},{8,13},{9,10},{10,... | collective-permute-start | bytes 196616 | tf_op jit(solution)/shard_map/ppermute | solution.py:171
  29.1 2.1 %collective-permute-done.13.got_ref = f32[64,256]{1,0:T(8,128)S(1)} collective-permute-done((f32[64,256]{1,0:T(8,128)S(1)}, f32[64,256]{1,0:T(8,128)S(1)}, u32[]{:S(2)}, u32[]{:S(2)}) %collective-permute-start.13) | collective-permute-done | bytes 65568 | tf_op jit(solution)/shard_map/ppermute | solution.py:171
  31.3 1.4 %collective-permute-start.14 = (f32[64,256]{1,0:T(8,128)S(1)}, f32[64,256]{1,0:T(8,128)S(1)}, u32[]{:S(2)}, u32[]{:S(2)}) collective-permute-start(f32[64,256]{1,0:T(8,128)S(1)} %shard_map.73.held_ref), channel_id=1, source_target_pairs={{0,17},{1,8},{2,11},{3,18},{4,13},{5,20},{6,23},{7,14},{8,1},{9,24... | collective-permute-start | bytes 196616 | tf_op jit(solution)/shard_map/ppermute | solution.py:171
  32.6 1.4 %collective-permute-done.22.got_ref = f32[64,256]{1,0:T(8,128)S(1)} collective-permute-done((f32[64,256]{1,0:T(8,128)S(1)}, f32[64,256]{1,0:T(8,128)S(1)}, u32[]{:S(2)}, u32[]{:S(2)}) %collective-permute-start.22) | collective-permute-done | bytes 65568 | tf_op jit(solution)/shard_map/ppermute | solution.py:171
  34.1 0.5 collective-permute-start.23
  34.6 0.6 %collective-permute-start.6 = (f32[128,256]{1,0:T(8,128)S(1)}, f32[128,256]{1,0:T(8,128)S(1)}, u32[]{:S(2)}, u32[]{:S(2)}) collective-permute-start(f32[128,256]{1,0:T(8,128)S(1)} %shard_map.65.held_ref), channel_id=1, source_target_pairs={{0,5},{1,16},{2,19},{3,6},{4,21},{5,0},{6,3},{7,22},{8,25},{9,12},... | collective-permute-start | bytes 393224 | tf_op jit(solution)/shard_map/ppermute | solution.py:171
  35.3 2.1 %collective-permute-start.15 = (f32[128,256]{1,0:T(8,128)S(1)}, f32[128,256]{1,0:T(8,128)S(1)}, u32[]{:S(2)}, u32[]{:S(2)}) collective-permute-start(f32[128,256]{1,0:T(8,128)S(1)} %shard_map.74.held_ref), channel_id=1, source_target_pairs={{0,5},{1,16},{2,19},{3,6},{4,21},{5,0},{6,3},{7,22},{8,25},{9,12},... | collective-permute-start | bytes 393224 | tf_op jit(solution)/shard_map/ppermute | solution.py:171
  37.4 0.4 collective-permute-done.23.got_ref
  37.8 1.8 %collective-permute-start.24 = (f32[128,256]{1,0:T(8,128)S(1)}, f32[128,256]{1,0:T(8,128)S(1)}, u32[]{:S(2)}, u32[]{:S(2)}) collective-permute-start(f32[128,256]{1,0:T(8,128)S(1)} %shard_map.83.held_ref), channel_id=1, source_target_pairs={{0,3},{1,4},{2,7},{3,0},{4,1},{5,6},{6,5},{7,2},{8,13},{9,10},{10,... | collective-permute-start | bytes 393224 | tf_op jit(solution)/shard_map/ppermute | solution.py:171
  39.6 1.8 %collective-permute-start.7 = (f32[256,256]{1,0:T(8,128)S(1)}, f32[256,256]{1,0:T(8,128)S(1)}, u32[]{:S(2)}, u32[]{:S(2)}) collective-permute-start(f32[256,256]{1,0:T(8,128)S(1)} %shard_map.66.held_ref), channel_id=1, source_target_pairs={{0,17},{1,2},{2,1},{3,18},{4,7},{5,20},{6,23},{7,4},{8,11},{9,24},... | collective-permute-start | bytes 786440 | tf_op jit(solution)/shard_map/ppermute | solution.py:171
  41.5 2.0 %collective-permute-start.16 = (f32[256,256]{1,0:T(8,128)S(1)}, f32[256,256]{1,0:T(8,128)S(1)}, u32[]{:S(2)}, u32[]{:S(2)}) collective-permute-start(f32[256,256]{1,0:T(8,128)S(1)} %shard_map.75.held_ref), channel_id=1, source_target_pairs={{0,3},{1,4},{2,7},{3,0},{4,1},{5,6},{6,5},{7,2},{8,13},{9,10},{10,... | collective-permute-start | bytes 786440 | tf_op jit(solution)/shard_map/ppermute | solution.py:171
  43.6 0.2 collective-permute-start.25
  43.8 3.1 %collective-permute-done.7.got_ref = f32[256,256]{1,0:T(8,128)S(1)} collective-permute-done((f32[256,256]{1,0:T(8,128)S(1)}, f32[256,256]{1,0:T(8,128)S(1)}, u32[]{:S(2)}, u32[]{:S(2)}) %collective-permute-start.7) | collective-permute-done | bytes 262176 | tf_op jit(solution)/shard_map/ppermute | solution.py:171
  46.9 0.1 shard_map.67.refs_0_
  47.0 3.6 %collective-permute-start.8 = (f32[512,256]{1,0:T(8,128)S(1)}, f32[512,256]{1,0:T(8,128)S(1)}, u32[]{:S(2)}, u32[]{:S(2)}) collective-permute-start(f32[512,256]{1,0:T(8,128)S(1)} %shard_map.67.refs_0_), channel_id=1, source_target_pairs={{0,1},{1,0},{2,3},{3,2},{4,5},{5,4},{6,7},{7,6},{8,9},{9,8},{10,11... | collective-permute-start | bytes 1572872 | tf_op jit(solution)/shard_map/ppermute | solution.py:171
  50.6 0.1 shard_map.76.refs_1_
  50.7 1.6 %collective-permute-start.17 = (f32[512,256]{1,0:T(8,128)S(1)}, f32[512,256]{1,0:T(8,128)S(1)}, u32[]{:S(2)}, u32[]{:S(2)}) collective-permute-start(f32[512,256]{1,0:T(8,128)S(1)} %shard_map.76.refs_1_), channel_id=1, source_target_pairs={{0,1},{1,0},{2,3},{3,2},{4,5},{5,4},{6,7},{7,6},{8,9},{9,8},{10,11... | collective-permute-start | bytes 1572872 | tf_op jit(solution)/shard_map/ppermute | solution.py:171
  52.2 0.1 shard_map.85.refs_2_
  52.3 0.1 collective-permute-start.26
  52.4 1.2 %shard_map.86 = (f32[1536,256]{1,0:T(8,128)}, f32[1536,256]{1,0:T(8,128)}) custom-call(f32[512,256]{1,0:T(8,128)S(1)} %shard_map.67.refs_0_, f32[512,256]{1,0:T(8,128)S(1)} %shard_map.76.refs_1_, f32[512,256]{1,0:T(8,128)S(1)} %shard_map.85.refs_2_), custom_call_target="tpu_custom_call" | custom-call | tf_op jit(solution)/shard_map/pallas_call | solution.py:72
  53.6 0.2 collective-permute-done.17.refs_1_
  53.8 0.7 %collective-permute-done.26.refs_2_ = f32[512,256]{1,0:T(8,128)S(1)} collective-permute-done((f32[512,256]{1,0:T(8,128)S(1)}, f32[512,256]{1,0:T(8,128)S(1)}, u32[]{:S(2)}, u32[]{:S(2)}) %collective-permute-start.26) | collective-permute-done | bytes 524320 | tf_op jit(solution)/shard_map/ppermute | solution.py:171
  54.5 1.2 %shard_map.87 = (f32[1536,256]{1,0:T(8,128)}, f32[1536,256]{1,0:T(8,128)}) custom-call(f32[512,256]{1,0:T(8,128)S(1)} %collective-permute-done.8.refs_0_, f32[512,256]{1,0:T(8,128)S(1)} %collective-permute-done.17.refs_1_, f32[512,256]{1,0:T(8,128)S(1)} %collective-permute-done.26.refs_2_, ...), custom_call_target="tpu_custom_call", output_to_operand_aliasing={{0}: (3, {}), {1}: (4, {})} | custom-call | tf_op jit(solution)/shard_map/pallas_call | solution.py:72
  (35 shorter events, 0.4 us)
Async XLA Ops:
  2.3 2.2 %collective-permute-start = (f32[512,256]{1,0:T(8,128)S(1)}, f32[512,256]{1,0:T(8,128)S(1)}, u32[]{:S(2)}, u32[]{:S(2)}) collective-permute-start(f32[512,256]{1,0:T(8,128)S(1)} %get-tuple-element.35), channel_id=1, source_target_pairs={{0,1},{1,0},{2,3},{3,2},{4,5},{5,4},{6,7},{7,6},{8,9},{9,8},{10,11... | collective-permute-start | bytes 1572872 | tf_op jit(solution)/shard_map/ppermute | solution.py:171
  3.2 4.0 %collective-permute-start.9 = (f32[512,256]{1,0:T(8,128)S(1)}, f32[512,256]{1,0:T(8,128)S(1)}, u32[]{:S(2)}, u32[]{:S(2)}) collective-permute-start(f32[512,256]{1,0:T(8,128)S(1)} %get-tuple-element.47), channel_id=1, source_target_pairs={{0,1},{1,0},{2,3},{3,2},{4,5},{5,4},{6,7},{7,6},{8,9},{9,8},{10,11... | collective-permute-start | bytes 1572872 | tf_op jit(solution)/shard_map/ppermute | solution.py:171
  3.9 4.8 %collective-permute-start.18 = (f32[512,256]{1,0:T(8,128)S(1)}, f32[512,256]{1,0:T(8,128)S(1)}, u32[]{:S(2)}, u32[]{:S(2)}) collective-permute-start(f32[512,256]{1,0:T(8,128)S(1)} %get-tuple-element.55), channel_id=1, source_target_pairs={{0,1},{1,0},{2,3},{3,2},{4,5},{5,4},{6,7},{7,6},{8,9},{9,8},{10,11... | collective-permute-start | bytes 1572872 | tf_op jit(solution)/shard_map/ppermute | solution.py:171
  4.5 6.7 %collective-permute-start.1 = (f32[256,256]{1,0:T(8,128)S(1)}, f32[256,256]{1,0:T(8,128)S(1)}, u32[]{:S(2)}, u32[]{:S(2)}) collective-permute-start(f32[256,256]{1,0:T(8,128)S(1)} %get-tuple-element.37), channel_id=1, source_target_pairs={{0,17},{1,2},{2,1},{3,18},{4,7},{5,20},{6,23},{7,4},{8,11},{9,24},... | collective-permute-start | bytes 786440 | tf_op jit(solution)/shard_map/ppermute | solution.py:171
  7.2 7.5 %collective-permute-start.10 = (f32[256,256]{1,0:T(8,128)S(1)}, f32[256,256]{1,0:T(8,128)S(1)}, u32[]{:S(2)}, u32[]{:S(2)}) collective-permute-start(f32[256,256]{1,0:T(8,128)S(1)} %get-tuple-element.49), channel_id=1, source_target_pairs={{0,3},{1,4},{2,7},{3,0},{4,1},{5,6},{6,5},{7,2},{8,13},{9,10},{10,... | collective-permute-start | bytes 786440 | tf_op jit(solution)/shard_map/ppermute | solution.py:171
  8.8 7.6 %collective-permute-start.19 = (f32[256,256]{1,0:T(8,128)S(1)}, f32[256,256]{1,0:T(8,128)S(1)}, u32[]{:S(2)}, u32[]{:S(2)}) collective-permute-start(f32[256,256]{1,0:T(8,128)S(1)} %get-tuple-element.57), channel_id=1, source_target_pairs={{0,5},{1,16},{2,19},{3,6},{4,21},{5,0},{6,3},{7,22},{8,25},{9,12},... | collective-permute-start | bytes 786440 | tf_op jit(solution)/shard_map/ppermute | solution.py:171
  11.3 6.6 %collective-permute-start.2 = (f32[128,256]{1,0:T(8,128)S(1)}, f32[128,256]{1,0:T(8,128)S(1)}, u32[]{:S(2)}, u32[]{:S(2)}) collective-permute-start(f32[128,256]{1,0:T(8,128)S(1)} %get-tuple-element.39), channel_id=1, source_target_pairs={{0,5},{1,16},{2,19},{3,6},{4,21},{5,0},{6,3},{7,22},{8,25},{9,12},... | collective-permute-start | bytes 393224 | tf_op jit(solution)/shard_map/ppermute | solution.py:171
  14.7 4.5 %collective-permute-start.11 = (f32[128,256]{1,0:T(8,128)S(1)}, f32[128,256]{1,0:T(8,128)S(1)}, u32[]{:S(2)}, u32[]{:S(2)}) collective-permute-start(f32[128,256]{1,0:T(8,128)S(1)} %get-tuple-element.51), channel_id=1, source_target_pairs={{0,5},{1,16},{2,19},{3,6},{4,21},{5,0},{6,3},{7,22},{8,25},{9,12},... | collective-permute-start | bytes 393224 | tf_op jit(solution)/shard_map/ppermute | solution.py:171
  16.4 4.7 %collective-permute-start.20 = (f32[128,256]{1,0:T(8,128)S(1)}, f32[128,256]{1,0:T(8,128)S(1)}, u32[]{:S(2)}, u32[]{:S(2)}) collective-permute-start(f32[128,256]{1,0:T(8,128)S(1)} %get-tuple-element.59), channel_id=1, source_target_pairs={{0,3},{1,4},{2,7},{3,0},{4,1},{5,6},{6,5},{7,2},{8,13},{9,10},{10,... | collective-permute-start | bytes 393224 | tf_op jit(solution)/shard_map/ppermute | solution.py:171
  17.9 4.4 %collective-permute-start.3 = (f32[64,256]{1,0:T(8,128)S(1)}, f32[64,256]{1,0:T(8,128)S(1)}, u32[]{:S(2)}, u32[]{:S(2)}) collective-permute-start(f32[64,256]{1,0:T(8,128)S(1)} %get-tuple-element.41), channel_id=1, source_target_pairs={{0,3},{1,4},{2,7},{3,0},{4,1},{5,6},{6,5},{7,2},{8,13},{9,10},{10,... | collective-permute-start | bytes 196616 | tf_op jit(solution)/shard_map/ppermute | solution.py:171
  19.2 5.6 %collective-permute-start.12 = (f32[64,256]{1,0:T(8,128)S(1)}, f32[64,256]{1,0:T(8,128)S(1)}, u32[]{:S(2)}, u32[]{:S(2)}) collective-permute-start(f32[64,256]{1,0:T(8,128)S(1)} %get-tuple-element.53), channel_id=1, source_target_pairs={{0,17},{1,8},{2,11},{3,18},{4,13},{5,20},{6,23},{7,14},{8,1},{9,24... | collective-permute-start | bytes 196616 | tf_op jit(solution)/shard_map/ppermute | solution.py:171
  21.2 4.5 %collective-permute-start.21 = (f32[64,256]{1,0:T(8,128)S(1)}, f32[64,256]{1,0:T(8,128)S(1)}, u32[]{:S(2)}, u32[]{:S(2)}) collective-permute-start(f32[64,256]{1,0:T(8,128)S(1)} %get-tuple-element.61), channel_id=1, source_target_pairs={{0,17},{1,2},{2,1},{3,18},{4,7},{5,20},{6,23},{7,4},{8,11},{9,24},... | collective-permute-start | bytes 196616 | tf_op jit(solution)/shard_map/ppermute | solution.py:171
  22.3 5.4 %collective-permute-start.4 = (f32[64,256]{1,0:T(8,128)S(1)}, f32[64,256]{1,0:T(8,128)S(1)}, u32[]{:S(2)}, u32[]{:S(2)}) collective-permute-start(f32[64,256]{1,0:T(8,128)S(1)} %shard_map.63.keep_ref), channel_id=1, source_target_pairs={{0,9},{1,8},{2,11},{3,10},{4,13},{5,12},{6,15},{7,14},{8,1},{9,0},... | collective-permute-start | bytes 196616 | tf_op jit(solution)/shard_map/ppermute | solution.py:171
  24.9 6.4 %collective-permute-start.13 = (f32[64,256]{1,0:T(8,128)S(1)}, f32[64,256]{1,0:T(8,128)S(1)}, u32[]{:S(2)}, u32[]{:S(2)}) collective-permute-start(f32[64,256]{1,0:T(8,128)S(1)} %shard_map.72.keep_ref), channel_id=1, source_target_pairs={{0,9},{1,2},{2,1},{3,10},{4,7},{5,12},{6,15},{7,4},{8,11},{9,0},{1... | collective-permute-start | bytes 196616 | tf_op jit(solution)/shard_map/ppermute | solution.py:171
  25.7 8.4 %collective-permute-start.22 = (f32[64,256]{1,0:T(8,128)S(1)}, f32[64,256]{1,0:T(8,128)S(1)}, u32[]{:S(2)}, u32[]{:S(2)}) collective-permute-start(f32[64,256]{1,0:T(8,128)S(1)} %shard_map.81.keep_ref), channel_id=1, source_target_pairs={{0,9},{1,8},{2,11},{3,10},{4,13},{5,12},{6,15},{7,14},{8,1},{9,0},... | collective-permute-start | bytes 196616 | tf_op jit(solution)/shard_map/ppermute | solution.py:171
  27.8 6.8 %collective-permute-start.5 = (f32[64,256]{1,0:T(8,128)S(1)}, f32[64,256]{1,0:T(8,128)S(1)}, u32[]{:S(2)}, u32[]{:S(2)}) collective-permute-start(f32[64,256]{1,0:T(8,128)S(1)} %shard_map.64.held_ref), channel_id=1, source_target_pairs={{0,3},{1,4},{2,7},{3,0},{4,1},{5,6},{6,5},{7,2},{8,13},{9,10},{10,... | collective-permute-start | bytes 196616 | tf_op jit(solution)/shard_map/ppermute | solution.py:171
  31.3 4.0 %collective-permute-start.14 = (f32[64,256]{1,0:T(8,128)S(1)}, f32[64,256]{1,0:T(8,128)S(1)}, u32[]{:S(2)}, u32[]{:S(2)}) collective-permute-start(f32[64,256]{1,0:T(8,128)S(1)} %shard_map.73.held_ref), channel_id=1, source_target_pairs={{0,17},{1,8},{2,11},{3,18},{4,13},{5,20},{6,23},{7,14},{8,1},{9,24... | collective-permute-start | bytes 196616 | tf_op jit(solution)/shard_map/ppermute | solution.py:171
  34.1 3.8 %collective-permute-start.23 = (f32[64,256]{1,0:T(8,128)S(1)}, f32[64,256]{1,0:T(8,128)S(1)}, u32[]{:S(2)}, u32[]{:S(2)}) collective-permute-start(f32[64,256]{1,0:T(8,128)S(1)} %shard_map.82.held_ref), channel_id=1, source_target_pairs={{0,17},{1,2},{2,1},{3,18},{4,7},{5,20},{6,23},{7,4},{8,11},{9,24},... | collective-permute-start | bytes 196616 | tf_op jit(solution)/shard_map/ppermute | solution.py:171
  34.6 5.0 %collective-permute-start.6 = (f32[128,256]{1,0:T(8,128)S(1)}, f32[128,256]{1,0:T(8,128)S(1)}, u32[]{:S(2)}, u32[]{:S(2)}) collective-permute-start(f32[128,256]{1,0:T(8,128)S(1)} %shard_map.65.held_ref), channel_id=1, source_target_pairs={{0,5},{1,16},{2,19},{3,6},{4,21},{5,0},{6,3},{7,22},{8,25},{9,12},... | collective-permute-start | bytes 393224 | tf_op jit(solution)/shard_map/ppermute | solution.py:171
  35.3 6.2 %collective-permute-start.15 = (f32[128,256]{1,0:T(8,128)S(1)}, f32[128,256]{1,0:T(8,128)S(1)}, u32[]{:S(2)}, u32[]{:S(2)}) collective-permute-start(f32[128,256]{1,0:T(8,128)S(1)} %shard_map.74.held_ref), channel_id=1, source_target_pairs={{0,5},{1,16},{2,19},{3,6},{4,21},{5,0},{6,3},{7,22},{8,25},{9,12},... | collective-permute-start | bytes 393224 | tf_op jit(solution)/shard_map/ppermute | solution.py:171
  37.8 5.7 %collective-permute-start.24 = (f32[128,256]{1,0:T(8,128)S(1)}, f32[128,256]{1,0:T(8,128)S(1)}, u32[]{:S(2)}, u32[]{:S(2)}) collective-permute-start(f32[128,256]{1,0:T(8,128)S(1)} %shard_map.83.held_ref), channel_id=1, source_target_pairs={{0,3},{1,4},{2,7},{3,0},{4,1},{5,6},{6,5},{7,2},{8,13},{9,10},{10,... | collective-permute-start | bytes 393224 | tf_op jit(solution)/shard_map/ppermute | solution.py:171
  39.6 7.3 %collective-permute-start.7 = (f32[256,256]{1,0:T(8,128)S(1)}, f32[256,256]{1,0:T(8,128)S(1)}, u32[]{:S(2)}, u32[]{:S(2)}) collective-permute-start(f32[256,256]{1,0:T(8,128)S(1)} %shard_map.66.held_ref), channel_id=1, source_target_pairs={{0,17},{1,2},{2,1},{3,18},{4,7},{5,20},{6,23},{7,4},{8,11},{9,24},... | collective-permute-start | bytes 786440 | tf_op jit(solution)/shard_map/ppermute | solution.py:171
  41.5 9.1 %collective-permute-start.16 = (f32[256,256]{1,0:T(8,128)S(1)}, f32[256,256]{1,0:T(8,128)S(1)}, u32[]{:S(2)}, u32[]{:S(2)}) collective-permute-start(f32[256,256]{1,0:T(8,128)S(1)} %shard_map.75.held_ref), channel_id=1, source_target_pairs={{0,3},{1,4},{2,7},{3,0},{4,1},{5,6},{6,5},{7,2},{8,13},{9,10},{10,... | collective-permute-start | bytes 786440 | tf_op jit(solution)/shard_map/ppermute | solution.py:171
  43.6 8.6 %collective-permute-start.25 = (f32[256,256]{1,0:T(8,128)S(1)}, f32[256,256]{1,0:T(8,128)S(1)}, u32[]{:S(2)}, u32[]{:S(2)}) collective-permute-start(f32[256,256]{1,0:T(8,128)S(1)} %shard_map.84.held_ref), channel_id=1, source_target_pairs={{0,5},{1,16},{2,19},{3,6},{4,21},{5,0},{6,3},{7,22},{8,25},{9,12},... | collective-permute-start | bytes 786440 | tf_op jit(solution)/shard_map/ppermute | solution.py:171
  47.0 6.6 %collective-permute-start.8 = (f32[512,256]{1,0:T(8,128)S(1)}, f32[512,256]{1,0:T(8,128)S(1)}, u32[]{:S(2)}, u32[]{:S(2)}) collective-permute-start(f32[512,256]{1,0:T(8,128)S(1)} %shard_map.67.refs_0_), channel_id=1, source_target_pairs={{0,1},{1,0},{2,3},{3,2},{4,5},{5,4},{6,7},{7,6},{8,9},{9,8},{10,11... | collective-permute-start | bytes 1572872 | tf_op jit(solution)/shard_map/ppermute | solution.py:171
  50.7 3.1 %collective-permute-start.17 = (f32[512,256]{1,0:T(8,128)S(1)}, f32[512,256]{1,0:T(8,128)S(1)}, u32[]{:S(2)}, u32[]{:S(2)}) collective-permute-start(f32[512,256]{1,0:T(8,128)S(1)} %shard_map.76.refs_1_), channel_id=1, source_target_pairs={{0,1},{1,0},{2,3},{3,2},{4,5},{5,4},{6,7},{7,6},{8,9},{9,8},{10,11... | collective-permute-start | bytes 1572872 | tf_op jit(solution)/shard_map/ppermute | solution.py:171
  52.3 2.2 %collective-permute-start.26 = (f32[512,256]{1,0:T(8,128)S(1)}, f32[512,256]{1,0:T(8,128)S(1)}, u32[]{:S(2)}, u32[]{:S(2)}) collective-permute-start(f32[512,256]{1,0:T(8,128)S(1)} %shard_map.85.refs_2_), channel_id=1, source_target_pairs={{0,1},{1,0},{2,3},{3,2},{4,5},{5,4},{6,7},{7,6},{8,9},{9,8},{10,11... | collective-permute-start | bytes 1572872 | tf_op jit(solution)/shard_map/ppermute | solution.py:171
